TPU v7x, 32 devices: a whole 2x2x4 slice. The times are simulated.
32 devices in a mesh: row: 8 (over y, x, core), col: 4 (over z).
Axes of the slice: x: 2, y: 2, z: 4, core: 2. Of those that a mesh axis runs over, the one named last changes fastest.
Arguments:
- inverse_blocks: bfloat16 [8, 384, 256, 256], P('row', 'col'), may hold values from -6 to 6
- inverse_rows: int32 [8, 384], P('row', 'col'), may hold values from 0 to 95, as said below
- inverse_cols: int32 [8, 384], P('row', 'col'), may hold values from 0 to 95, as said below
- inverse_count: int32 [8, 4], P('row', 'col'), may hold values from 1 to 96, as said below
- panel_rows: int32 [16], replicated, may hold values from -1 to 95, as said below
- lower_old: bfloat16 [3, 16, 256, 256], P(None, 'row'), may hold values from -0.038085938 to 0.038085938
- lower_new: bfloat16 [3, 3, 256, 256], replicated, may hold values from -0.375 to 0.375
- diag_inverse: float32 [3, 256, 256], replicated, may hold values from -6 to 6
Outputs:
- panel_inverse: bfloat16 [3, 16, 256, 256], P(None, 'row', 'col')
- supernode_inverse: float32 [3, 3, 256, 256], replicated
Inputs may be any that keep to these rules, and one draw needn't show every extreme that they name: `panel_rows`: for each row index r in order, 2 entries: distinct block rows congruent to r modulo the number of row indices, at least one, then -1 in the empty slots; some row index fills all 2 in every draw. `inverse_rows`: on row index r every slot names one of the panel rows of r, padding slots too. `inverse_cols`: on column index c every slot names a block column congruent to c modulo the number of column indices; positions may repeat, and repeated blocks add. `inverse_count`: slots 0 to count - 1 of a device's lists are live, the rest padding; one device reaches 96 in every draw.
All inputs are finite; a program needn't handle non-finite values.
Results may differ from a plain program's by a relative error of at most 0.0045.
Values may be sent and summed in bfloat16 or wider, within the bound.
No kernel may reach another device: no remote copies, remote signals or barrier semaphores. Data moves between devices by JAX's collectives and lax.ppermute only.
A program may use at most 128 MiB of HBM per device.

v0:
```python
import jax
import jax.numpy as jnp
from jax import lax
from jax.sharding import PartitionSpec as P

exact_mode = lax.Precision.HIGHEST
group_size = 8


def partner_2(value, axis, distance):
    mask = 2**distance
    pairs = [(source, source ^ mask) for source in range(lax.axis_size(axis))]
    return lax.ppermute(value, axis, pairs)


def linked(blocks_new, left_node, right_node):
    if left_node == right_node:
        return blocks_new[left_node, left_node]
    if right_node > left_node:
        return blocks_new[right_node, left_node]
    return blocks_new[left_node, right_node].T


def per_device(
    inverse_blocks,
    inverse_rows,
    inverse_cols,
    inverse_count,
    panel_rows,
    lower_old,
    lower_new,
    diag_inverse,
):
    blocks = inverse_blocks[0]
    stored_rows = inverse_rows[0]
    stored_cols = inverse_cols[0]
    stored_count = inverse_count[0, 0]
    supernodes = lower_old.shape[0]
    slot_count = lower_old.shape[1]
    block_width = blocks.shape[-1]
    row_devs = lax.axis_size("row")
    col_devs = lax.axis_size("col")
    row_me = lax.axis_index("row")
    col_me = lax.axis_index("col")
    own_rows = lax.dynamic_slice_in_dim(panel_rows, row_me * slot_count, slot_count)
    holding = lower_old
    for bit_index in range(col_devs.bit_length() - 1):
        partner = partner_2(holding, "row", bit_index)
        differ = row_me >> bit_index & 1 != col_me >> bit_index & 1
        holding = jnp.where(differ, partner, holding)
    for bit_index in range(col_devs.bit_length() - 1, row_devs.bit_length() - 1):
        partner = partner_2(holding, "row", bit_index)
        upper_half = row_me >> bit_index & 1 == 1
        holding = jnp.where(
            upper_half,
            jnp.concatenate([partner, holding], axis=1),
            jnp.concatenate([holding, partner], axis=1),
        )
    candidates = holding
    sources = jnp.arange(row_devs // col_devs, dtype=jnp.int32) * col_devs + col_me
    cand_rows = panel_rows.reshape(row_devs, slot_count)[sources].reshape(-1)
    cand_index = jnp.arange(cand_rows.shape[0], dtype=jnp.int32)

    def accumulate(group_index, running):
        offset = group_index * group_size
        block_part = lax.dynamic_slice_in_dim(blocks, offset, group_size)
        row_part = lax.dynamic_slice_in_dim(stored_rows, offset, group_size)
        col_part = lax.dynamic_slice_in_dim(stored_cols, offset, group_size)
        is_live = offset + jnp.arange(group_size, dtype=jnp.int32) < stored_count
        matches = col_part[:, None] == cand_rows[None, :]
        present = jnp.any(matches, axis=1) & is_live
        position = jnp.sum(jnp.where(matches, cand_index[None, :], 0), axis=1)
        factors = jnp.take(candidates, position, axis=1)
        products = jnp.einsum(
            "kab,skbc->skac", block_part, factors, preferred_element_type=jnp.float32
        )
        target = ((row_part[:, None] == own_rows[None, :]) & present[:, None]).astype(jnp.float32)
        return running + jnp.einsum("ks,tkac->tsac", target, products, precision=exact_mode)

    partial_value = lax.fori_loop(
        0,
        (stored_count + group_size - 1) // group_size,
        accumulate,
        jnp.zeros((supernodes, slot_count, block_width, block_width), jnp.float32),
    )
    share_rows = block_width // col_devs
    base_part = lax.psum(partial_value, "col")
    lower_links = lower_new.astype(jnp.float32)
    panels = []
    blocks_new = {}
    for node in range(supernodes):
        running = base_part[node]
        for earlier in range(node):
            running = running + jnp.einsum(
                "sab,bc->sac",
                panels[earlier],
                lower_new[node, earlier],
                preferred_element_type=jnp.float32,
            )
        current = (-running).astype(jnp.bfloat16)
        lower_step = lower_old[node]
        term_list = [
            jnp.einsum(
                "sab,sac->bc", panels[earlier], lower_step, preferred_element_type=jnp.float32
            )
            for earlier in range(node)
        ]
        term_list.append(
            jnp.einsum("sab,sac->bc", lower_step, current, preferred_element_type=jnp.float32)
        )
        summed = lax.psum(jnp.stack(term_list), "row")
        for earlier in range(node):
            crossed = summed[earlier]
            for another in range(node):
                crossed = crossed + jnp.dot(
                    linked(blocks_new, earlier, another),
                    lower_links[node, another],
                    precision=exact_mode,
                )
            blocks_new[node, earlier] = -crossed
        diagonal_block = diag_inverse[node] - summed[node]
        for earlier in range(node):
            diagonal_block = diagonal_block - jnp.dot(
                lower_links[node, earlier].T, blocks_new[node, earlier], precision=exact_mode
            )
        blocks_new[node, node] = diagonal_block
        panels.append(current)
    stacked = jnp.stack(panels)
    panel_inverse = lax.dynamic_slice_in_dim(stacked, col_me * share_rows, share_rows, 2)
    empty_block = jnp.zeros((block_width, block_width), jnp.float32)
    supernode_inverse = jnp.stack(
        [
            jnp.stack(
                [
                    blocks_new[node, earlier] if earlier <= node else empty_block
                    for earlier in range(supernodes)
                ]
            )
            for node in range(supernodes)
        ]
    )
    return (panel_inverse, supernode_inverse)


def solution(mesh):
    placed = (
        P("row", "col", None, None),
        P("row", "col"),
        P("row", "col"),
        P("row", "col"),
        P(),
        P(None, "row", None, None),
        P(),
        P(),
    )
    return jax.shard_map(
        per_device,
        mesh=mesh,
        in_specs=placed,
        out_specs=(P(None, "row", "col", None), P()),
        check_vma=False,
    )
```

profile of v0, /device:TPU:0, one launch (start us, length us, event | category | flops | bytes accessed | tf_op | source)
XLA Modules:
  0.0 490.5 jit_solution(17268165076970064919)
XLA Ops:
  7.8 2.1 collective-permute-done
  9.9 1.2 broadcast_select_fusion
  11.1 2.9 collective-permute-start.1
  14.0 16.7 %collective-permute-done.1 = bf16[3,2,256,256]{3,2,1,0:T(8,128)(2,1)S(1)} collective-permute-done((bf16[3,2,256,256]{3,2,1,0:T(8,128)(2,1)S(1)}, bf16[3,2,256,256]{3,2,1,0:T(8,128)(2,1)S(1)}, u32[]{:S(2)}, u32[]{:S(2)}) %collective-permute-start.1) | collective-permute-done | bytes 786464 | tf_op jit(solution)/shard_map/ppermute | solution.py:13
  30.8 1.8 collective-permute-start.2
  34.2 14.6 %collective-permute-done.2 = bf16[3,2,256,256]{3,2,1,0:T(8,128)(2,1)S(1)} collective-permute-done((bf16[3,2,256,256]{3,2,1,0:T(8,128)(2,1)S(1)}, bf16[3,2,256,256]{3,2,1,0:T(8,128)(2,1)S(1)}, u32[]{:S(2)}, u32[]{:S(2)}) %collective-permute-start.2) | collective-permute-done | bytes 786464 | tf_op jit(solution)/shard_map/ppermute | solution.py:13
  48.8 1.4 maximum_select_fusion
  50.2 1.5 broadcast_in_dim.31
  51.8 47.7 %while.12 = (s32[]{:T(128)}, f32[3,2,256,256]{3,1,2,0:T(2,128)}, s32[]{:T(128)}, s32[96]{0:T(128)S(1)}, s32[2,2]{1,0:T(2,128)}, /*index=5*/bf16[3,4,256,256]{3,2...) while((s32[]{:T(128)}, f32[3,2,256,256]{3,1,2,0:T(2,128)}, ...), condition=%wide.wide.region_3.4_spmd.clone, body=%wide.wide.region_0.3_spmd.clone.sunk | while | flops 845022464 | bytes 51385088 | solution.py:80
  51.9 2.2 gather_fusion
  54.1 5.1 %fusion.112 = f32[3,8,256,256]{2,3,0,1:T(8,128)} fusion(bf16[8,3,256,256]{3,2,1,0:T(8,128)(2,1)S(1)} %gather_fusion, pred[8]{0:T(512)(128)(4,1)S(1)} %compare_and_fusion.6, bf16[96,256,256]{2,1,0:T(8,128)(2,1)} %get-tuple-element.263, s32[]{:T(128)S(6)} %select_n.126), kind=kOutput, calls=%fused_computation.7.clone.clone.1 | convolution fusion | flops 806879232 | bytes 10485772 | tf_op jit(solution)/shard_map/while/body/kab,skbc->skac/dot_general | solution.py:74
  59.2 6.8 %copy.94 = f32[3,8,256,256]{3,1,2,0:T(8,128)} copy(f32[3,8,256,256]{2,3,0,1:T(8,128)} %fusion.112) | data formatting | bytes 12582912 | tf_op jit(solution)/shard_map/while/body/kab,skbc->skac/transpose | solution.py:74
  66.8 7.6 %bitcast_add_fusion.3 = f32[3,2,256,256]{3,1,2,0:T(2,128)S(1)} fusion(f32[3,2,256,256]{3,1,2,0:T(2,128)S(1)} %copy-done, f32[3,8,256,256]{3,1,2,0:T(8,128)} %copy.94, pred[8]{0:T(512)(128)(4,1)S(1)} %compare_and_fusion.7, s32[8]{0:T(128)S(1)} %dynamic_slice.46, s32[2]{0:T(128)S(1)} %get-tuple-element.265), kind=kOutput, calls=%fused_computation.8.clone.clone.1 | convolution fusion | flops 38141984 | bytes 9437232 | tf_op jit(solution)/shard_map/while/body/ks,tkac->tsac/dot_general | solution.py:78
  75.8 2.2 gather_fusion
  77.9 5.1 %fusion.112 = f32[3,8,256,256]{2,3,0,1:T(8,128)} fusion(bf16[8,3,256,256]{3,2,1,0:T(8,128)(2,1)S(1)} %gather_fusion, pred[8]{0:T(512)(128)(4,1)S(1)} %compare_and_fusion.6, bf16[96,256,256]{2,1,0:T(8,128)(2,1)} %get-tuple-element.263, s32[]{:T(128)S(6)} %select_n.126), kind=kOutput, calls=%fused_computation.7.clone.clone.1 | convolution fusion | flops 806879232 | bytes 10485772 | tf_op jit(solution)/shard_map/while/body/kab,skbc->skac/dot_general | solution.py:74
  83.1 6.8 %copy.94 = f32[3,8,256,256]{3,1,2,0:T(8,128)} copy(f32[3,8,256,256]{2,3,0,1:T(8,128)} %fusion.112) | data formatting | bytes 12582912 | tf_op jit(solution)/shard_map/while/body/kab,skbc->skac/transpose | solution.py:74
  90.7 7.6 %bitcast_add_fusion.3 = f32[3,2,256,256]{3,1,2,0:T(2,128)S(1)} fusion(f32[3,2,256,256]{3,1,2,0:T(2,128)S(1)} %copy-done, f32[3,8,256,256]{3,1,2,0:T(8,128)} %copy.94, pred[8]{0:T(512)(128)(4,1)S(1)} %compare_and_fusion.7, s32[8]{0:T(128)S(1)} %dynamic_slice.46, s32[2]{0:T(128)S(1)} %get-tuple-element.265), kind=kOutput, calls=%fused_computation.8.clone.clone.1 | convolution fusion | flops 38141984 | bytes 9437232 | tf_op jit(solution)/shard_map/while/body/ks,tkac->tsac/dot_general | solution.py:78
  99.4 2.7 copy.50
  102.4 309.0 %all-reduce.5.cloned.1.call-done = f32[3,2,256,256]{3,2,1,0:T(8,128)} async-done(((f32[3,2,256,256]{3,2,1,0:T(8,128)}), f32[3,2,256,256]{3,2,1,0:T(8,128)}) %all-reduce.5.cloned.1.call-update) | async-done | bytes 1572880 | tf_op jit(solution)/shard_map/psum | solution.py:87
  412.8 1.3 fusion.24
  415.9 1.3 convolution_add_fusion.1
  419.5 1.2 fusion.80
  421.8 56.0 %all-reduce.7.cloned.1.call-done = (f32[3,256,256]{1,2,0:T(8,128)}, f32[1,256,256]{1,2,0:T(8,128)}, f32[2,256,256]{1,2,0:T(8,128)}) async-done(((f32[3,256,256]{1,2,0:T(8,128)}, f32[1,256,256]{1,2,0:T(8,128)}, f32[2,256,256]{1,2,0:T(8,128)}), (f32[3,256,256]{1,2,0:T(8,128)}, f32[1,256,256]{1,2,0:T(8,128)}, f32[2,256,256]{1,2,0:T(8,128)})) %all-reduce.7.cloned.1.call-update) | async-done | bytes 1572880 | tf_op jit(solution)/shard_map/psum | solution.py:111
  481.7 2.0 copy.68
  (79 shorter events, 16.4 us)
Async XLA Ops:
  7.2 404.2 %all-reduce.5.cloned.1.call-start = ((), (), s32[]{:S(2)}) async-start(), calls=%async_computation | async-start | bytes 3145728 | tf_op jit(solution)/shard_map/psum | solution.py:87
  7.2 2.7 collective-permute-start
  11.1 22.2 %copy-start.7 = (s32[16]{0:T(128)S(1)}, s32[16]{0:T(128)}, u32[]{:S(2)}) copy-start(s32[16]{0:T(128)} %param.14) | copy-start | bytes 196
  11.1 19.6 %collective-permute-start.1 = (bf16[3,2,256,256]{3,2,1,0:T(8,128)(2,1)S(1)}, bf16[3,2,256,256]{3,2,1,0:T(8,128)(2,1)S(1)}, u32[]{:S(2)}, u32[]{:S(2)}) collective-permute-start(bf16[3,2,256,256]{3,2,1,0:T(8,128)(2,1)S(1)} %broadcast_select_fusion), channel_id=1, source_target_pairs={{0,8},{4,12},{8,0},{12,4},{16,24},{20,28},{24,16},{28,20},{1,9},{5... | collective-permute-start | bytes 2359304 | tf_op jit(solution)/shard_map/ppermute | solution.py:13
  30.8 17.9 %collective-permute-start.2 = (bf16[3,2,256,256]{3,2,1,0:T(8,128)(2,1)S(1)}, bf16[3,2,256,256]{3,2,1,0:T(8,128)(2,1)S(1)}, u32[]{:S(2)}, u32[]{:S(2)}) collective-permute-start(bf16[3,2,256,256]{3,2,1,0:T(8,128)(2,1)S(1)} %broadcast_select_fusion.1), channel_id=1, source_target_pairs={{0,16},{4,20},{8,24},{12,28},{16,0},{20,4},{24,8},{28,12},{1,17},{... | collective-permute-start | bytes 2359304 | tf_op jit(solution)/shard_map/ppermute | solution.py:13
  34.1 16.1 %copy-start.6 = (s32[2,2]{1,0:T(2,128)}, s32[2,2]{1,0:T(2,128)S(1)}, u32[]{:S(2)}) copy-start(s32[2,2]{1,0:T(2,128)S(1)} %gather_fusion.1) | copy-start | bytes 52
  50.2 1.6 copy-start.8
  50.2 1.6 copy-start.9
  59.2 7.6 %copy-start = (f32[3,2,256,256]{3,1,2,0:T(2,128)S(1)}, f32[3,2,256,256]{3,1,2,0:T(2,128)}, u32[]{:S(2)}) copy-start(f32[3,2,256,256]{3,1,2,0:T(2,128)} %get-tuple-element.243) | copy-start | bytes 4718596 | tf_op jit(solution)/shard_map/while
  74.4 1.1 copy-start.1
  83.1 7.6 %copy-start = (f32[3,2,256,256]{3,1,2,0:T(2,128)S(1)}, f32[3,2,256,256]{3,1,2,0:T(2,128)}, u32[]{:S(2)}) copy-start(f32[3,2,256,256]{3,1,2,0:T(2,128)} %get-tuple-element.243) | copy-start | bytes 4718596 | tf_op jit(solution)/shard_map/while
  98.3 1.1 copy-start.1
  102.2 310.3 %copy-start.2 = (bf16[3,2,256,256]{3,2,1,0:T(8,128)(2,1)S(1)}, bf16[3,2,256,256]{3,2,1,0:T(8,128)(2,1)}, u32[]{:S(2)}) copy-start(bf16[3,2,256,256]{3,2,1,0:T(8,128)(2,1)} %param.15) | copy-start | bytes 2359300
  102.2 310.6 %copy-start.3 = (bf16[3,3,256,256]{3,2,1,0:T(8,128)(2,1)S(1)}, bf16[3,3,256,256]{3,2,1,0:T(8,128)(2,1)}, u32[]{:S(2)}) copy-start(bf16[3,3,256,256]{3,2,1,0:T(8,128)(2,1)} %param.16) | copy-start | bytes 3538948
  102.2 375.6 %all-reduce.7.cloned.1.call-start = ((), (), s32[]{:S(2)}) async-start(), calls=%async_computation.1 | async-start | bytes 3145728 | tf_op jit(solution)/shard_map/psum | solution.py:111
  477.8 1.2 copy-start.5
  477.8 1.5 copy-start.4
Sparse Core Ops, SparseCore 0:
  102.3 309.0 all-reduce.4
  419.6 58.1 all-reduce.6
where the time goes:
time: 493 us; the launch traced here: 490 us
  waiting for transfers between devices  398 us (81%)
  matrix products  32.9 us (7%)
  local copies, waits for them, and re-layouts  29.2 us (6%)
  between operations  15 us (3%)
  other arithmetic  9.31 us (2%)
  starting transfers between devices  5.56 us (1%)
    psum x1, waiting for transfers between devices, per_device(): base_part = lax.psum(partial_value, 'col')  309 us
    psum x1, waiting for transfers between devices, per_device(): summed = lax.psum(jnp.stack(term_list), 'row')  56 us
    ppermute x3, waiting for transfers between devices, partner_2(): return lax.ppermute(value, axis, pairs)  33.4 us
    dot_general x2, matrix products, accumulate(): jnp.einsum('ks,tkac->tsac', target, products, precision=exact_mode)  15.2 us
    transpose x2, local copies, waits for them, and re-layouts, accumulate(): jnp.einsum('kab,skbc->skac', block_part, factors, preferred_element_type=...  13.6 us
    dot_general x2, matrix products, accumulate(): jnp.einsum('kab,skbc->skac', block_part, factors, preferred_element_type=...  10.2 us
  transfers between devices with their start and end apart: 5, of which 5 were waited for; matrix products, arithmetic and copies ran while one was open for 1% of the time, Pallas kernels for 0%

commit v1 on v0

--- a/solution.py
+++ b/solution.py
@@ -84,7 +84,7 @@
         jnp.zeros((supernodes, slot_count, block_width, block_width), jnp.float32),
     )
     share_rows = block_width // col_devs
-    base_part = lax.psum(partial_value, "col")
+    base_part = jnp.sum(lax.all_gather(partial_value, "col"), axis=0)
     lower_links = lower_new.astype(jnp.float32)
     panels = []
     blocks_new = {}

time: 493 us -> 541 us (1.097)
  waiting for transfers between devices: 398 us -> 444 us
    all_gather x0 -> x1, waiting for transfers between devices: none -> 355 us  [per_device(): base_part = jnp.sum(lax.all_gather(partial_value, 'col'), axis=0)]
    psum x1 -> x0, waiting for transfers between devices: 309 us -> none  [per_device(): base_part = lax.psum(partial_value, 'col')]
  transfers between devices with their start and end apart: 5 -> 5, of which waited for: 5 -> 5; matrix products, arithmetic and copies ran while one was open for 1% -> 0% of each run, Pallas kernels for 0% -> 0%
where the time goes in v1:
time: 541 us; the launch traced here: 539 us
  waiting for transfers between devices  444 us (82%)
  matrix products  33.5 us (6%)
  local copies, waits for them, and re-layouts  28.6 us (5%)
  between operations  15 us (3%)
  other arithmetic  11.7 us (2%)
  starting transfers between devices  5.56 us (1%)
    all_gather x1, waiting for transfers between devices, per_device(): base_part = jnp.sum(lax.all_gather(partial_value, 'col'), axis=0)  355 us
    psum x1, waiting for transfers between devices, per_device(): summed = lax.psum(jnp.stack(term_list), 'row')  55.7 us
    ppermute x3, waiting for transfers between devices, partner_2(): return lax.ppermute(value, axis, pairs)  33.4 us
    dot_general x2, matrix products, accumulate(): jnp.einsum('ks,tkac->tsac', target, products, precision=exact_mode)  15.2 us
    transpose x2, local copies, waits for them, and re-layouts, accumulate(): jnp.einsum('kab,skbc->skac', block_part, factors, preferred_element_type=...  13.6 us
  transfers between devices with their start and end apart: 5, of which 5 were waited for; matrix products, arithmetic and copies ran while one was open for 0% of the time, Pallas kernels for 0%

profile of v1, /device:TPU:0, one launch (start us, length us, event | category | flops | bytes accessed | tf_op | source)
XLA Modules:
  0.0 538.9 jit_solution(14985960354779314915)
XLA Ops:
  7.8 2.1 collective-permute-done
  9.9 1.2 broadcast_select_fusion
  11.1 2.9 collective-permute-start.1
  14.0 16.7 %collective-permute-done.1 = bf16[3,2,256,256]{3,2,1,0:T(8,128)(2,1)S(1)} collective-permute-done((bf16[3,2,256,256]{3,2,1,0:T(8,128)(2,1)S(1)}, bf16[3,2,256,256]{3,2,1,0:T(8,128)(2,1)S(1)}, u32[]{:S(2)}, u32[]{:S(2)}) %collective-permute-start.1) | collective-permute-done | bytes 786464 | tf_op jit(solution)/shard_map/ppermute | solution.py:13
  30.8 1.8 collective-permute-start.2
  34.2 14.6 %collective-permute-done.2 = bf16[3,2,256,256]{3,2,1,0:T(8,128)(2,1)S(1)} collective-permute-done((bf16[3,2,256,256]{3,2,1,0:T(8,128)(2,1)S(1)}, bf16[3,2,256,256]{3,2,1,0:T(8,128)(2,1)S(1)}, u32[]{:S(2)}, u32[]{:S(2)}) %collective-permute-start.2) | collective-permute-done | bytes 786464 | tf_op jit(solution)/shard_map/ppermute | solution.py:13
  48.8 1.4 maximum_select_fusion
  50.2 1.5 broadcast_in_dim.31
  51.7 47.7 %while.12 = (s32[]{:T(128)}, f32[3,2,256,256]{3,1,2,0:T(2,128)}, s32[]{:T(128)}, s32[96]{0:T(128)S(1)}, s32[2,2]{1,0:T(2,128)}, /*index=5*/bf16[3,4,256,256]{3,2...) while((s32[]{:T(128)}, f32[3,2,256,256]{3,1,2,0:T(2,128)}, ...), condition=%wide.wide.region_3.4_spmd.clone, body=%wide.wide.region_0.3_spmd.clone.sunk | while | flops 845022464 | bytes 51385088 | solution.py:80
  51.9 2.2 gather_fusion
  54.1 5.1 fusion.112
  59.2 6.8 %copy.128 = f32[3,8,256,256]{3,1,2,0:T(8,128)} copy(f32[3,8,256,256]{2,3,0,1:T(8,128)} %fusion.112) | data formatting | bytes 12582912 | tf_op jit(solution)/shard_map/while/body/kab,skbc->skac/transpose | solution.py:74
  66.8 7.6 %bitcast_add_fusion.3 = f32[3,2,256,256]{3,1,2,0:T(2,128)S(1)} fusion(f32[3,2,256,256]{3,1,2,0:T(2,128)S(1)} %copy-done, f32[3,8,256,256]{3,1,2,0:T(8,128)} %copy.128, pred[8]{0:T(512)(128)(4,1)S(1)} %compare_and_fusion.7, s32[8]{0:T(128)S(1)} %dynamic_slice.46, s32[2]{0:T(128)S(1)} %get-tuple-element.267), kind=kOutput, calls=%fused_computation.8.clone.clone.1 | convolution fusion | flops 38141984 | bytes 9437232 | tf_op jit(solution)/shard_map/while/body/ks,tkac->tsac/dot_general | solution.py:78
  74.4 1.1 copy-done.1
  75.8 2.2 gather_fusion
  77.9 5.1 fusion.112
  83.0 6.8 %copy.128 = f32[3,8,256,256]{3,1,2,0:T(8,128)} copy(f32[3,8,256,256]{2,3,0,1:T(8,128)} %fusion.112) | data formatting | bytes 12582912 | tf_op jit(solution)/shard_map/while/body/kab,skbc->skac/transpose | solution.py:74
  90.7 7.6 %bitcast_add_fusion.3 = f32[3,2,256,256]{3,1,2,0:T(2,128)S(1)} fusion(f32[3,2,256,256]{3,1,2,0:T(2,128)S(1)} %copy-done, f32[3,8,256,256]{3,1,2,0:T(8,128)} %copy.128, pred[8]{0:T(512)(128)(4,1)S(1)} %compare_and_fusion.7, s32[8]{0:T(128)S(1)} %dynamic_slice.46, s32[2]{0:T(128)S(1)} %get-tuple-element.267), kind=kOutput, calls=%fused_computation.8.clone.clone.1 | convolution fusion | flops 38141984 | bytes 9437232 | tf_op jit(solution)/shard_map/while/body/ks,tkac->tsac/dot_general | solution.py:78
  98.3 1.1 copy-done.1
  99.4 2.7 copy.73
  102.4 355.3 %all-gather.3.cloned.1.call-done = f32[12,2,256,256]{3,2,1,0:T(8,128)} async-done(((f32[3,2,256,256]{3,2,1,0:T(8,128)}), f32[12,2,256,256]{3,2,1,0:T(8,128)}) %all-gather.3.cloned.1.call-update) | async-done | bytes 6291472 | tf_op jit(solution)/shard_map/all_gather | solution.py:87
  457.7 3.5 reduce_sum.20
  470.4 55.7 %all-reduce.4.cloned.1.call-done = (f32[3,256,256]{1,2,0:T(8,128)}, f32[1,256,256]{1,2,0:T(8,128)}, f32[2,256,256]{1,2,0:T(8,128)}) async-done(((f32[3,256,256]{1,2,0:T(8,128)}, f32[1,256,256]{1,2,0:T(8,128)}, f32[2,256,256]{1,2,0:T(8,128)}), (f32[3,256,256]{1,2,0:T(8,128)}, f32[1,256,256]{1,2,0:T(8,128)}, f32[2,256,256]{1,2,0:T(8,128)})) %all-reduce.4.cloned.1.call-update) | async-done | bytes 1572880 | tf_op jit(solution)/shard_map/psum | solution.py:111
  530.1 2.0 copy.95
  (82 shorter events, 16.8 us)
Async XLA Ops:
  7.2 450.5 %all-gather.3.cloned.1.call-start = ((), (), s32[]{:S(2)}) async-start(), calls=%async_computation | async-start | bytes 7864320 | tf_op jit(solution)/shard_map/all_gather | solution.py:87
  7.2 2.7 collective-permute-start
  11.1 22.2 %copy-start.8 = (s32[16]{0:T(128)S(1)}, s32[16]{0:T(128)}, u32[]{:S(2)}) copy-start(s32[16]{0:T(128)} %param.14) | copy-start | bytes 196
  11.1 19.6 %collective-permute-start.1 = (bf16[3,2,256,256]{3,2,1,0:T(8,128)(2,1)S(1)}, bf16[3,2,256,256]{3,2,1,0:T(8,128)(2,1)S(1)}, u32[]{:S(2)}, u32[]{:S(2)}) collective-permute-start(bf16[3,2,256,256]{3,2,1,0:T(8,128)(2,1)S(1)} %broadcast_select_fusion), channel_id=1, source_target_pairs={{0,8},{4,12},{8,0},{12,4},{16,24},{20,28},{24,16},{28,20},{1,9},{5... | collective-permute-start | bytes 2359304 | tf_op jit(solution)/shard_map/ppermute | solution.py:13
  30.8 17.9 %collective-permute-start.2 = (bf16[3,2,256,256]{3,2,1,0:T(8,128)(2,1)S(1)}, bf16[3,2,256,256]{3,2,1,0:T(8,128)(2,1)S(1)}, u32[]{:S(2)}, u32[]{:S(2)}) collective-permute-start(bf16[3,2,256,256]{3,2,1,0:T(8,128)(2,1)S(1)} %broadcast_select_fusion.1), channel_id=1, source_target_pairs={{0,16},{4,20},{8,24},{12,28},{16,0},{20,4},{24,8},{28,12},{1,17},{... | collective-permute-start | bytes 2359304 | tf_op jit(solution)/shard_map/ppermute | solution.py:13
  34.1 16.1 %copy-start.7 = (s32[2,2]{1,0:T(2,128)}, s32[2,2]{1,0:T(2,128)S(1)}, u32[]{:S(2)}) copy-start(s32[2,2]{1,0:T(2,128)S(1)} %gather_fusion.1) | copy-start | bytes 52
  50.2 1.6 copy-start.9
  50.2 1.6 copy-start.10
  59.2 7.6 %copy-start = (f32[3,2,256,256]{3,1,2,0:T(2,128)S(1)}, f32[3,2,256,256]{3,1,2,0:T(2,128)}, u32[]{:S(2)}) copy-start(f32[3,2,256,256]{3,1,2,0:T(2,128)} %get-tuple-element.245) | copy-start | bytes 4718596 | tf_op jit(solution)/shard_map/while
  74.4 1.1 copy-start.1
  83.0 7.6 %copy-start = (f32[3,2,256,256]{3,1,2,0:T(2,128)S(1)}, f32[3,2,256,256]{3,1,2,0:T(2,128)}, u32[]{:S(2)}) copy-start(f32[3,2,256,256]{3,1,2,0:T(2,128)} %get-tuple-element.245) | copy-start | bytes 4718596 | tf_op jit(solution)/shard_map/while
  98.3 1.1 copy-start.1
  102.1 424.0 %all-reduce.4.cloned.1.call-start = ((), (), s32[]{:S(2)}) async-start(), calls=%async_computation.1 | async-start | bytes 3145728 | tf_op jit(solution)/shard_map/psum | solution.py:111
  457.7 3.5 copy-start.2
  467.8 1.4 copy-start.4
  469.5 57.8 %copy-start.3 = (bf16[3,3,256,256]{3,2,1,0:T(8,128)(2,1)S(1)}, bf16[3,3,256,256]{3,2,1,0:T(8,128)(2,1)}, u32[]{:S(2)}) copy-start(bf16[3,3,256,256]{3,2,1,0:T(8,128)(2,1)} %param.16) | copy-start | bytes 3538948
  526.2 1.2 copy-start.6
  526.2 1.5 copy-start.5
Sparse Core Ops, SparseCore 0:
  102.3 355.3 all-gather.2
  468.9 57.2 all-reduce.3
